TPU v7x, 32 devices: a whole 2x2x4 slice. The times are simulated.
32 devices in a mesh: runs: 2 (over x), space: 16 (over z, y, core).
Axes of the slice: x: 2, y: 2, z: 4, core: 2. Of those that a mesh axis runs over, the one named last changes fastest.
Arguments:
- fields: float32 [128, 512], P(('runs', 'space')), parts along dimension 0, may hold values from -3 to 3
- end_weights: bfloat16 [256, 128, 512], P(None, ('runs', 'space')), parts along dimension 1, may hold values from 0.5 to 1.5
- directions: float32 [3, 256], replicated, may hold values from -1 to 1
- analysis: bfloat16 [256, 256], replicated, may hold values from -0.375 to 0.375
- synthesis: bfloat16 [256, 256], replicated, may hold values from -0.375 to 0.375
- decay_rates: float32 [256], replicated, may hold values from 0.1 to 1
Outputs:
- density: float32 [128, 512], P(('runs', 'space')), parts along dimension 0
There are 2 independent parts, one for each index of `runs`. A program takes and returns all parts, laid end to end along the dimension named above; an argument that names none is the same for every part. Nothing has to cross between parts.
All inputs are finite; a program needn't handle non-finite values.
Results may differ from a plain program's by a relative error of at most 0.003.
Values may be sent and summed in bfloat16 or wider, within the bound.
A program may use at most 64 MiB of HBM per device.

v0:
```python
import functools

import jax
import jax.numpy as jnp
from jax import lax
from jax.experimental import pallas as pl
from jax.experimental.pallas import tpu as pltpu
from jax.sharding import PartitionSpec as P

NZ = 16
STEPS = 4
HALF = STEPS // 2
YB = 4

courant = 0.3
slope = 0.6

MESH = pl.DeviceIdType.MESH
F32 = jnp.float32
BF16 = jnp.bfloat16


def lane_sum(product):
    width = product.shape[1]
    half = width // 2
    folded = product[:, :half] + product[:, half:]
    high = folded.astype(BF16)
    low = (folded - high.astype(F32)).astype(BF16)
    both = jnp.concatenate([high, low], axis=1)
    ones = jnp.ones((8, width), BF16)
    total = lax.dot_general(ones, both, (((1,), (1,)), ((), ())), preferred_element_type=F32)
    return total[0:1]


def kernel(
    devices, chunk, fields, ends, directions, analysis, synthesis, decay, out,
    state, moved, edges, mixing, column, coef, field_in, half_out,
    x_out, x_in, y_out, y_in, reduced, part_out, part_in, rho_out, rho_in,
    field_sem, ends_sem, x_send, x_recv, y_send, y_recv, part_send, part_recv, rho_sem,
):
    planes, cells = fields.shape
    half_cells = cells // 2
    rows = half_cells // NZ
    orient = directions.shape[1]
    inner = range(1, planes - 1)
    last = planes - 1
    count = rows // chunk
    order = list(range(1, count - 1)) + [0, count - 1]
    me = lax.axis_index("space")
    team = lax.rem(me, 2)
    partner = me + 1 - 2 * team
    after = lax.rem(me + 2, devices)
    before = lax.rem(me + devices - 2, devices)

    barrier = pltpu.get_barrier_semaphore()

    @pl.loop(1, devices)
    def _(d):
        pl.semaphore_signal(
            barrier, inc=1, device_id={"space": lax.rem(me + d, devices)}, device_id_type=MESH
        )

    def remote(source, target, send, recv, device):
        return pltpu.make_async_remote_copy(
            src_ref=source, dst_ref=target, send_sem=send, recv_sem=recv,
            device_id={"space": device}, device_id_type=MESH,
        )

    def wide(factor):
        return jnp.concatenate([factor] * (orient // 128), axis=-1)

    def my_half(ref):
        return jnp.where(team == 0, ref[:, :half_cells], ref[:, half_cells:])

    def upright(row):
        return jnp.broadcast_to(row, (128, half_cells)).T.reshape(rows, NZ, 128)

    sign = (1 - 2 * team).astype(F32)
    speed = sign * directions[...]
    pos = courant * jnp.maximum(speed, 0.0)
    neg = courant * jnp.maximum(-speed, 0.0)
    stay = 1.0 - jnp.sum(pos + neg, axis=0, keepdims=True)
    for c in range(3):
        coef[0, c:c + 1] = pos[c:c + 1]
        coef[0, 3 + c:4 + c] = neg[c:c + 1]
        coef[1, c:c + 1] = neg[c:c + 1]
        coef[1, 3 + c:4 + c] = pos[c:c + 1]
    coef[0, 6:7] = stay
    coef[1, 6:7] = stay

    own_at = pl.multiple_of(team * half_cells, half_cells)
    other_at = pl.multiple_of((1 - team) * half_cells, half_cells)
    plane_at = me // 2 * planes + lax.broadcasted_iota(jnp.int32, (planes, 1), 0)
    ramp = slope * plane_at.astype(F32) / (planes * (devices // 2))
    w_own = my_half(fields) + ramp
    w_away = jnp.where(team == 0, fields[:, half_cells:], fields[:, :half_cells]) + ramp
    factor_own = jnp.exp(-0.5 * w_own)
    factor_away = jnp.exp(-0.5 * w_away)
    def prepare(i):
        away = ends[i, pl.ds(other_at, half_cells)].astype(F32).reshape(rows, NZ, orient)
        half_out[i] = (wide(upright(factor_away[i:i + 1])) * away).astype(BF16)
        column[0, i] = upright(factor_own[i:i + 1])
        own = ends[i, pl.ds(own_at, half_cells)].astype(F32).reshape(rows, NZ, orient)
        state[0, 0, i] = (wide(column[0, i]) * own).astype(BF16)

    for i in (last, 0):
        prepare(i)

    pl.semaphore_wait(barrier, devices - 1)

    field_copy = remote(fields, field_in, field_sem.at[0], field_sem.at[1], partner)

    def ends_copy(i, k=0, low=0, size=rows):
        at = pl.ds(low, size)
        return remote(
            half_out.at[i, at], state.at[1, 0, i, at],
            ends_sem.at[0, i, k], ends_sem.at[1, i, k], partner,
        )

    for k in order:
        ends_copy(last, k, k * chunk, chunk).start()
        ends_copy(0, k, k * chunk, chunk).start()
    field_copy.start()
    def x_copy(s, side, k):
        at = pl.ds(k * chunk, chunk)
        return remote(
            x_out.at[s, side, at], x_in.at[s, side, at],
            x_send.at[s, side, k], x_recv.at[s, side, k],
            after if side == 0 else before,
        )

    spans = ((1, planes - 2), (0, 1), (last, 1))

    def y_copy(s, side, span):
        at = pl.ds(*spans[span])
        return remote(
            y_out.at[s, side, at], y_in.at[s, side, at],
            y_send.at[s, side, span], y_recv.at[s, side, span], partner,
        )

    def packed(first, second, c):
        forward = coef[0, c:c + 1].reshape(1, 1, orient) > 0.0
        return jnp.where(forward, first.astype(F32), second.astype(F32)).astype(BF16)

    def send_y(s, span):
        low, size = spans[span]
        at = slice(low, low + size)
        y_out[s, 0, at] = packed(state[0, s, at, rows - 1], state[1, s, at, rows - 1], 1)
        y_copy(s, 0, span).start()
        y_out[s, 1, at] = packed(state[1, s, at, 0], state[0, s, at, 0], 1)
        y_copy(s, 1, span).start()

    def wait_y(s, span):
        y_copy(s, 0, span).wait()
        y_copy(s, 1, span).wait()

    def drift(s, sp, i, y, size):
        def weight(k):
            return coef[sp, k:k + 1].reshape(1, 1, orient)

        def part(ref, low, high):
            return ref[low:high].astype(F32)

        here = state.at[sp, s, i]
        center = part(here, y, y + size)
        x_before = x_in.at[s, 0] if i == 0 else state.at[sp, s, i - 1]
        x_after = x_in.at[s, 1] if i == last else state.at[sp, s, i + 1]
        if y == 0:
            y_before = jnp.concatenate(
                [y_in[s, 0, i].astype(F32)[None], part(here, 0, size - 1)], axis=0
            )
        else:
            y_before = part(here, y - 1, y + size - 1)
        if y + size == rows:
            y_after = jnp.concatenate(
                [part(here, y + 1, rows), y_in[s, 1, i].astype(F32)[None]], axis=0
            )
        else:
            y_after = part(here, y + 1, y + size + 1)
        total = weight(6) * center
        total = total + weight(0) * part(x_before, y, y + size)
        total = total + weight(3) * part(x_after, y, y + size)
        total = total + weight(1) * y_before
        total = total + weight(4) * y_after
        total = total + weight(2) * pltpu.roll(center, 1, 1)
        total = total + weight(5) * pltpu.roll(center, NZ - 1, 1)
        return total.astype(BF16)

    def mix(block):
        shape = block.shape
        flat = block.reshape(shape[0] * NZ, orient)
        return jnp.dot(flat, mixing[...], preferred_element_type=F32).reshape(shape)

    def growth(s, sp, i, low, high):
        now = sp if s < HALF else 1 - sp
        then = sp if s + 1 < HALF else 1 - sp
        return wide(column[now, i, low:high] * column[then, i, low:high])

    def advance(s, sp, i):
        for y in range(0, rows, YB):
            moved[y:y + YB] = drift(s, sp, i, y, YB)
        state[sp, s + 1, i] = (growth(s, sp, i, 0, rows) * mix(moved[...])).astype(BF16)

    corners = ((0, last), (1, last), (0, 0), (1, 0))

    def boundary(s, k):
        y = k * chunk
        for n, (sp, i) in enumerate(corners):
            edges[n * chunk:(n + 1) * chunk] = drift(s, sp, i, y, chunk)
        mixed = mix(edges[...])
        grown = []
        for n, (sp, i) in enumerate(corners):
            value = growth(s, sp, i, y, y + chunk) * mixed[n * chunk:(n + 1) * chunk]
            state[sp, s + 1, i, y:y + chunk] = value.astype(BF16)
            grown.append(value)
        if s + 1 < STEPS:
            x_out[s + 1, 0, y:y + chunk] = packed(grown[0], grown[1], 0)
            x_copy(s + 1, 0, k).start()
            x_out[s + 1, 1, y:y + chunk] = packed(grown[3], grown[2], 0)
            x_copy(s + 1, 1, k).start()

    def pair(k, sp, s, sq, t, i):
        product = state[sp, s, i].astype(F32) * state[sq, t, i].astype(F32)
        reduced[k, i] = lane_sum(product.reshape(half_cells, orient))

    def term(k):
        return jnp.concatenate([reduced[k, i] for i in range(planes)], axis=0)

    for k in order:
        for i, side, first in ((last, 0, 0), (0, 1, 1)):
            ends_copy(i, k, k * chunk, chunk).wait()
            at = slice(k * chunk, (k + 1) * chunk)
            x_out[0, side, at] = packed(state[first, 0, i, at], state[1 - first, 0, i, at], 0)
            x_copy(0, side, k).start()
    send_y(0, 1)
    send_y(0, 2)
    for i in inner:
        prepare(i)
        ends_copy(i).start()

    scaled = synthesis[...].astype(F32) * decay[...]
    high = scaled.astype(BF16)
    low = (scaled - high.astype(F32)).astype(BF16)
    matrix = jnp.dot(high, analysis[...], preferred_element_type=F32)
    matrix = matrix + jnp.dot(low, analysis[...], preferred_element_type=F32)
    mixing[...] = (matrix.T + 1.0 / orient).astype(BF16)

    for i in inner:
        ends_copy(i).wait()
    send_y(0, 0)
    field_copy.wait()
    w_other = my_half(field_in) + ramp
    factor_other = jnp.exp(-0.5 * w_other)
    for i in range(planes):
        column[1, i] = upright(factor_other[i:i + 1])

    def part_copy(d):
        return remote(
            part_out, part_in.at[d], part_send.at[d], part_recv.at[d], lax.rem(me + d, devices)
        )

    def middle():
        return jnp.exp(0.5 * (w_own + w_other)) * term(0)

    def send_part():
        local = jnp.sum(middle(), axis=0, keepdims=True)
        local = sum(local[:, k:k + 128] for k in range(0, half_cells, 128))
        part_out[...] = local
        part_in[0] = local

        @pl.loop(1, devices)
        def _(d):
            part_copy(d).start()

    for s in range(STEPS):
        wait_y(s, 0)
        inside = [functools.partial(advance, s, sp, i) for i in inner for sp in (0, 1)]
        if s + 1 < STEPS:
            inside.append(functools.partial(send_y, s + 1, 0))
        work = list(inside)
        if s == HALF:
            early = [functools.partial(pair, 0, 0, HALF, 1, HALF, i) for i in range(planes)]
            work = early + [send_part] + inside
        if s == STEPS - 1:
            for i in range(planes):
                work.append(functools.partial(pair, 1, 0, 1, 1, 3, i))
                work.append(functools.partial(pair, 2, 1, 1, 0, 3, i))
            for i in inner:
                work.append(functools.partial(pair, 3, 0, 0, 1, 4, i))
                work.append(functools.partial(pair, 4, 1, 0, 0, 4, i))
        for n, k in enumerate(order):
            for task in work[n * len(work) // count:(n + 1) * len(work) // count]:
                task()
            if k == 0:
                wait_y(s, 1)
                wait_y(s, 2)
            x_copy(s, 0, k).wait()
            x_copy(s, 1, k).wait()
            boundary(s, k)
        if s + 1 < STEPS:
            send_y(s + 1, 1)
            send_y(s + 1, 2)

    for i in (0, last):
        pair(3, 0, 0, 1, 4, i)
        pair(4, 1, 0, 0, 4, i)

    @pl.loop(1, devices)
    def _(d):
        part_copy(d).wait()

    whole = jnp.sum(jnp.sum(part_in[...], axis=0), axis=1, keepdims=True)
    inverse = (planes * cells * (devices // 2)) / whole

    rho_other = jnp.exp(w_other) * (0.5 * term(4) + term(2)) + 0.5 * middle()
    rho_out[...] = rho_other * inverse
    rho_copy = remote(rho_out, rho_in, rho_sem.at[0], rho_sem.at[1], partner)
    rho_copy.start()
    rho_own = jnp.exp(w_own) * (0.5 * term(3) + term(1)) + 0.5 * middle()
    kept = rho_own * inverse
    rho_copy.wait()
    got = rho_in[...]
    out[:, :half_cells] = jnp.where(team == 0, kept, got)
    out[:, half_cells:] = jnp.where(team == 0, got, kept)


def shards(fields, end_weights, directions, analysis, synthesis, decay_rates):
    devices = lax.axis_size("space")
    planes, cells = fields.shape
    orient = end_weights.shape[0]
    half_cells = cells // 2
    rows = half_cells // NZ
    chunk = rows // 4
    ends = jnp.transpose(end_weights, (1, 2, 0))
    dma = pltpu.SemaphoreType.DMA
    vmem = pl.BlockSpec(memory_space=pltpu.VMEM)
    return pl.pallas_call(
        functools.partial(kernel, devices, chunk),
        out_shape=jax.ShapeDtypeStruct((planes, cells), F32),
        in_specs=[vmem] * 6,
        out_specs=vmem,
        scratch_shapes=[
            pltpu.VMEM((2, STEPS + 1, planes, rows, NZ, orient), BF16),
            pltpu.VMEM((rows, NZ, orient), BF16),
            pltpu.VMEM((4 * chunk, NZ, orient), BF16),
            pltpu.VMEM((orient, orient), BF16),
            pltpu.VMEM((2, planes, rows, NZ, 128), F32),
            pltpu.VMEM((2, 8, orient), F32),
            pltpu.VMEM((planes, cells), F32),
            pltpu.VMEM((planes, rows, NZ, orient), BF16),
            pltpu.VMEM((STEPS, 2, rows, NZ, orient), BF16),
            pltpu.VMEM((STEPS, 2, rows, NZ, orient), BF16),
            pltpu.VMEM((STEPS, 2, planes, NZ, orient), BF16),
            pltpu.VMEM((STEPS, 2, planes, NZ, orient), BF16),
            pltpu.VMEM((5, planes, 1, half_cells), F32),
            pltpu.VMEM((1, 128), F32),
            pltpu.VMEM((devices, 1, 128), F32),
            pltpu.VMEM((planes, half_cells), F32),
            pltpu.VMEM((planes, half_cells), F32),
            dma((2,)),
            dma((2, planes, rows // chunk)),
            dma((STEPS, 2, rows // chunk)),
            dma((STEPS, 2, rows // chunk)),
            dma((STEPS, 2, 3)),
            dma((STEPS, 2, 3)),
            dma((devices,)),
            dma((devices,)),
            dma((2,)),
        ],
        compiler_params=pltpu.CompilerParams(
            collective_id=0, has_side_effects=True, vmem_limit_bytes=32 * 1024 * 1024
        ),
        name="propagate",
    )(fields, ends, directions, analysis, synthesis, decay_rates.reshape(1, -1))


def solution(mesh):
    return jax.shard_map(
        shards,
        mesh=mesh,
        in_specs=(P(("runs", "space"), None), P(None, ("runs", "space"), None), P(), P(), P(), P()),
        out_specs=P(("runs", "space"), None),
        check_vma=False,
    )
```

profile of v0, /device:TPU:0, one launch (start us, length us, event | category | flops | bytes accessed | tf_op | source)
XLA Modules:
  0.0 38.5 jit_solution(14466649739230729812)
XLA Ops:
  0.0 0.0 copy-start
  0.0 0.0 copy-start.1
  0.0 0.0 copy-start.2
  0.0 0.0 copy-start.3
  0.0 1.7 %copy.7 = bf16[256,4,512]{0,2,1:T(8,128)(2,1)S(1)} copy(bf16[256,4,512]{2,1,0:T(4,128)(2,1)} %param.7) | data formatting | bytes 2097152 | tf_op args[1]
  1.7 0.0 copy-start.4
  1.7 0.0 copy-done
  1.7 0.0 copy-done.1
  1.7 0.0 copy-done.2
  1.7 0.0 copy-done.3
  1.7 0.6 %copy-done.4 = f32[256]{0:T(256)S(1)} copy-done((f32[256]{0:T(256)S(1)}, f32[256]{0:T(256)}, u32[]{:S(2)}) %copy-start.4) | copy-done | bytes 1048
  2.4 35.5 %propagate.1 = f32[4,512]{1,0:T(4,128)S(1)} custom-call(f32[4,512]{1,0:T(4,128)S(1)} %copy-done.2, bf16[4,512,256]{2,1,0:T(8,128)(2,1)S(1)} %bitcast.2, f32[3,256]{1,0:T(4,128)S(1)} %copy-done.3, bf16[256,256]{1,0:T(8,128)(2,1)S(1)} %copy-done, bf16[256,256]{1,0:T(8,128)(2,1)S(1)} %copy-done.1, f32[1,256]{1,0:T(1,128)S(1)} %bitcast.3), custom_call_target="tpu_custom_call" | custom-call | tf_op jit(solution)/shard_map/propagate/pallas_call | solution.py:337
  37.9 0.6 %copy.9 = f32[4,512]{1,0:T(4,128)} copy(f32[4,512]{1,0:T(4,128)S(1)} %propagate.1) | data formatting | bytes 16384
Async XLA Ops:
  0.0 1.7 %copy-start = (bf16[256,256]{1,0:T(8,128)(2,1)S(1)}, bf16[256,256]{1,0:T(8,128)(2,1)}, u32[]{:S(2)}) copy-start(bf16[256,256]{1,0:T(8,128)(2,1)} %analysis.1) | copy-start | bytes 393220
  0.0 1.7 %copy-start.1 = (bf16[256,256]{1,0:T(8,128)(2,1)S(1)}, bf16[256,256]{1,0:T(8,128)(2,1)}, u32[]{:S(2)}) copy-start(bf16[256,256]{1,0:T(8,128)(2,1)} %synthesis.1) | copy-start | bytes 393220
  0.0 1.7 %copy-start.2 = (f32[4,512]{1,0:T(4,128)S(1)}, f32[4,512]{1,0:T(4,128)}, u32[]{:S(2)}) copy-start(f32[4,512]{1,0:T(4,128)} %fields.1) | copy-start | bytes 24580
  0.0 1.7 %copy-start.3 = (f32[3,256]{1,0:T(4,128)S(1)}, f32[3,256]{1,0:T(4,128)}, u32[]{:S(2)}) copy-start(f32[3,256]{1,0:T(4,128)} %directions.1) | copy-start | bytes 9220
  1.7 0.7 %copy-start.4 = (f32[256]{0:T(256)S(1)}, f32[256]{0:T(256)}, u32[]{:S(2)}) copy-start(f32[256]{0:T(256)} %param.11) | copy-start | bytes 3076
where the time goes:
time: 38.6 us; the launch traced here: 38.5 us
  Pallas kernels  35.5 us (92%)
  local copies, waits for them, and re-layouts  2.92 us (8%)
    pallas_call x1, Pallas kernels, shards(): pl.pallas_call(functools.partial(kernel, devices, chunk), out_shape=jax.S...  35.5 us
    unnamed x12, local copies, waits for them, and re-layouts  2.92 us

commit v1 on v0

--- a/solution.py
+++ b/solution.py
@@ -21,14 +21,8 @@
 
 
 def lane_sum(product):
-    width = product.shape[1]
-    half = width // 2
-    folded = product[:, :half] + product[:, half:]
-    high = folded.astype(BF16)
-    low = (folded - high.astype(F32)).astype(BF16)
-    both = jnp.concatenate([high, low], axis=1)
-    ones = jnp.ones((8, width), BF16)
-    total = lax.dot_general(ones, both, (((1,), (1,)), ((), ())), preferred_element_type=F32)
+    ones = jnp.ones((8, product.shape[1]), BF16)
+    total = lax.dot_general(ones, product, (((1,), (1,)), ((), ())), preferred_element_type=F32)
     return total[0:1]
 
 
@@ -156,10 +150,10 @@
 
     def drift(s, sp, i, y, size):
         def weight(k):
-            return coef[sp, k:k + 1].reshape(1, 1, orient)
+            return coef[sp, k:k + 1].astype(BF16).reshape(1, 1, orient)
 
         def part(ref, low, high):
-            return ref[low:high].astype(F32)
+            return ref[low:high]
 
         here = state.at[sp, s, i]
         center = part(here, y, y + size)
@@ -167,13 +161,13 @@
         x_after = x_in.at[s, 1] if i == last else state.at[sp, s, i + 1]
         if y == 0:
             y_before = jnp.concatenate(
-                [y_in[s, 0, i].astype(F32)[None], part(here, 0, size - 1)], axis=0
+                [y_in[s, 0, i][None], part(here, 0, size - 1)], axis=0
             )
         else:
             y_before = part(here, y - 1, y + size - 1)
         if y + size == rows:
             y_after = jnp.concatenate(
-                [part(here, y + 1, rows), y_in[s, 1, i].astype(F32)[None]], axis=0
+                [part(here, y + 1, rows), y_in[s, 1, i][None]], axis=0
             )
         else:
             y_after = part(here, y + 1, y + size + 1)
@@ -220,7 +214,7 @@
             x_copy(s + 1, 1, k).start()
 
     def pair(k, sp, s, sq, t, i):
-        product = state[sp, s, i].astype(F32) * state[sq, t, i].astype(F32)
+        product = state[sp, s, i] * state[sq, t, i]
         reduced[k, i] = lane_sum(product.reshape(half_cells, orient))
 
     def term(k):
@@ -238,7 +232,7 @@
         prepare(i)
         ends_copy(i).start()
 
-    scaled = synthesis[...].astype(F32) * decay[...]
+    scaled = synthesis[...].astype(F32) * decay[...].reshape(1, orient)
     high = scaled.astype(BF16)
     low = (scaled - high.astype(F32)).astype(BF16)
     matrix = jnp.dot(high, analysis[...], preferred_element_type=F32)
@@ -289,14 +283,14 @@
                 work.append(functools.partial(pair, 3, 0, 0, 1, 4, i))
                 work.append(functools.partial(pair, 4, 1, 0, 0, 4, i))
         for n, k in enumerate(order):
-            for task in work[n * len(work) // count:(n + 1) * len(work) // count]:
-                task()
             if k == 0:
                 wait_y(s, 1)
                 wait_y(s, 2)
             x_copy(s, 0, k).wait()
             x_copy(s, 1, k).wait()
             boundary(s, k)
+            for task in work[n * len(work) // count:(n + 1) * len(work) // count]:
+                task()
         if s + 1 < STEPS:
             send_y(s + 1, 1)
             send_y(s + 1, 2)
@@ -371,7 +365,7 @@
             collective_id=0, has_side_effects=True, vmem_limit_bytes=32 * 1024 * 1024
         ),
         name="propagate",
-    )(fields, ends, directions, analysis, synthesis, decay_rates.reshape(1, -1))
+    )(fields, ends, directions, analysis, synthesis, decay_rates)
 
 
 def solution(mesh):

time: 38.6 us -> 38.3 us (level)
  no operation moved by 1% of the time
where the time goes in v1:
time: 38.3 us; the launch traced here: 38.2 us
  Pallas kernels  35.2 us (92%)
  local copies, waits for them, and re-layouts  2.92 us (8%)
    pallas_call x1, Pallas kernels, shards(): pl.pallas_call(functools.partial(kernel, devices, chunk), out_shape=jax.S...  35.2 us
    unnamed x12, local copies, waits for them, and re-layouts  2.92 us

profile of v1, /device:TPU:0, one launch (start us, length us, event | category | flops | bytes accessed | tf_op | source)
XLA Modules:
  0.0 38.2 jit_solution(11021613274491508063)
XLA Ops:
  0.0 0.0 copy-start.1
  0.0 0.0 copy-start
  0.0 0.0 copy-start.2
  0.0 0.0 copy-start.3
  0.0 1.7 %copy.7 = bf16[256,4,512]{0,2,1:T(8,128)(2,1)S(1)} copy(bf16[256,4,512]{2,1,0:T(4,128)(2,1)} %param.7) | data formatting | bytes 2097152 | tf_op args[1]
  1.7 0.0 copy-start.4
  1.7 0.0 copy-done.1
  1.7 0.0 copy-done
  1.7 0.0 copy-done.2
  1.7 0.0 copy-done.3
  1.7 0.6 %copy-done.4 = f32[256]{0:T(256)S(1)} copy-done((f32[256]{0:T(256)S(1)}, f32[256]{0:T(256)}, u32[]{:S(2)}) %copy-start.4) | copy-done | bytes 1048
  2.4 35.2 %propagate.1 = f32[4,512]{1,0:T(4,128)S(1)} custom-call(f32[4,512]{1,0:T(4,128)S(1)} %copy-done.2, bf16[4,512,256]{2,1,0:T(8,128)(2,1)S(1)} %bitcast.1, f32[3,256]{1,0:T(4,128)S(1)} %copy-done.3, bf16[256,256]{1,0:T(8,128)(2,1)S(1)} %copy-done, bf16[256,256]{1,0:T(8,128)(2,1)S(1)} %copy-done.1, f32[256]{0:T(256)S(1)} %copy-done.4), custom_call_target="tpu_custom_call" | custom-call | tf_op jit(solution)/shard_map/propagate/pallas_call | solution.py:331
  37.6 0.6 %copy.9 = f32[4,512]{1,0:T(4,128)} copy(f32[4,512]{1,0:T(4,128)S(1)} %propagate.1) | data formatting | bytes 16384
Async XLA Ops:
  0.0 1.7 %copy-start.1 = (bf16[256,256]{1,0:T(8,128)(2,1)S(1)}, bf16[256,256]{1,0:T(8,128)(2,1)}, u32[]{:S(2)}) copy-start(bf16[256,256]{1,0:T(8,128)(2,1)} %synthesis.1) | copy-start | bytes 393220
  0.0 1.7 %copy-start = (bf16[256,256]{1,0:T(8,128)(2,1)S(1)}, bf16[256,256]{1,0:T(8,128)(2,1)}, u32[]{:S(2)}) copy-start(bf16[256,256]{1,0:T(8,128)(2,1)} %analysis.1) | copy-start | bytes 393220
  0.0 1.7 %copy-start.2 = (f32[4,512]{1,0:T(4,128)S(1)}, f32[4,512]{1,0:T(4,128)}, u32[]{:S(2)}) copy-start(f32[4,512]{1,0:T(4,128)} %fields.1) | copy-start | bytes 24580
  0.0 1.7 %copy-start.3 = (f32[3,256]{1,0:T(4,128)S(1)}, f32[3,256]{1,0:T(4,128)}, u32[]{:S(2)}) copy-start(f32[3,256]{1,0:T(4,128)} %directions.1) | copy-start | bytes 9220
  1.7 0.7 %copy-start.4 = (f32[256]{0:T(256)S(1)}, f32[256]{0:T(256)}, u32[]{:S(2)}) copy-start(f32[256]{0:T(256)} %decay.1) | copy-start | bytes 3076

commit v2 on v1

--- a/solution.py
+++ b/solution.py
@@ -90,15 +90,18 @@
     w_away = jnp.where(team == 0, fields[:, half_cells:], fields[:, :half_cells]) + ramp
     factor_own = jnp.exp(-0.5 * w_own)
     factor_away = jnp.exp(-0.5 * w_away)
-    def prepare(i):
+
+    def prepare_away(i):
         away = ends[i, pl.ds(other_at, half_cells)].astype(F32).reshape(rows, NZ, orient)
         half_out[i] = (wide(upright(factor_away[i:i + 1])) * away).astype(BF16)
+
+    def prepare_own(i):
         column[0, i] = upright(factor_own[i:i + 1])
         own = ends[i, pl.ds(own_at, half_cells)].astype(F32).reshape(rows, NZ, orient)
         state[0, 0, i] = (wide(column[0, i]) * own).astype(BF16)
 
     for i in (last, 0):
-        prepare(i)
+        prepare_away(i)
 
     pl.semaphore_wait(barrier, devices - 1)
 
@@ -115,6 +118,9 @@
         ends_copy(last, k, k * chunk, chunk).start()
         ends_copy(0, k, k * chunk, chunk).start()
     field_copy.start()
+    for i in (last, 0):
+        prepare_own(i)
+
     def x_copy(s, side, k):
         at = pl.ds(k * chunk, chunk)
         return remote(
@@ -229,8 +235,9 @@
     send_y(0, 1)
     send_y(0, 2)
     for i in inner:
-        prepare(i)
+        prepare_away(i)
         ends_copy(i).start()
+        prepare_own(i)
 
     scaled = synthesis[...].astype(F32) * decay[...].reshape(1, orient)
     high = scaled.astype(BF16)

time: 38.3 us -> 38.3 us (level)
  no operation moved by 1% of the time
where the time goes in v2:
time: 38.3 us; the launch traced here: 38.2 us
  Pallas kernels  35.2 us (92%)
  local copies, waits for them, and re-layouts  2.92 us (8%)
    pallas_call x1, Pallas kernels, shards(): pl.pallas_call(functools.partial(kernel, devices, chunk), out_shape=jax.S...  35.2 us
    unnamed x12, local copies, waits for them, and re-layouts  2.92 us

profile of v2, /device:TPU:0, one launch (start us, length us, event | category | flops | bytes accessed | tf_op | source)
XLA Modules:
  0.0 38.2 jit_solution(1499156320976762216)
XLA Ops:
  0.0 0.0 copy-start.1
  0.0 0.0 copy-start
  0.0 0.0 copy-start.2
  0.0 0.0 copy-start.3
  0.0 1.7 %copy.7 = bf16[256,4,512]{0,2,1:T(8,128)(2,1)S(1)} copy(bf16[256,4,512]{2,1,0:T(4,128)(2,1)} %param.7) | data formatting | bytes 2097152 | tf_op args[1]
  1.7 0.0 copy-start.4
  1.7 0.0 copy-done.1
  1.7 0.0 copy-done
  1.7 0.0 copy-done.2
  1.7 0.0 copy-done.3
  1.7 0.6 %copy-done.4 = f32[256]{0:T(256)S(1)} copy-done((f32[256]{0:T(256)S(1)}, f32[256]{0:T(256)}, u32[]{:S(2)}) %copy-start.4) | copy-done | bytes 1048
  2.4 35.2 %propagate.1 = f32[4,512]{1,0:T(4,128)S(1)} custom-call(f32[4,512]{1,0:T(4,128)S(1)} %copy-done.2, bf16[4,512,256]{2,1,0:T(8,128)(2,1)S(1)} %bitcast.1, f32[3,256]{1,0:T(4,128)S(1)} %copy-done.3, bf16[256,256]{1,0:T(8,128)(2,1)S(1)} %copy-done, bf16[256,256]{1,0:T(8,128)(2,1)S(1)} %copy-done.1, f32[256]{0:T(256)S(1)} %copy-done.4), custom_call_target="tpu_custom_call" | custom-call | tf_op jit(solution)/shard_map/propagate/pallas_call | solution.py:338
  37.6 0.6 %copy.9 = f32[4,512]{1,0:T(4,128)} copy(f32[4,512]{1,0:T(4,128)S(1)} %propagate.1) | data formatting | bytes 16384
Async XLA Ops:
  0.0 1.7 %copy-start.1 = (bf16[256,256]{1,0:T(8,128)(2,1)S(1)}, bf16[256,256]{1,0:T(8,128)(2,1)}, u32[]{:S(2)}) copy-start(bf16[256,256]{1,0:T(8,128)(2,1)} %synthesis.1) | copy-start | bytes 393220
  0.0 1.7 %copy-start = (bf16[256,256]{1,0:T(8,128)(2,1)S(1)}, bf16[256,256]{1,0:T(8,128)(2,1)}, u32[]{:S(2)}) copy-start(bf16[256,256]{1,0:T(8,128)(2,1)} %analysis.1) | copy-start | bytes 393220
  0.0 1.7 %copy-start.2 = (f32[4,512]{1,0:T(4,128)S(1)}, f32[4,512]{1,0:T(4,128)}, u32[]{:S(2)}) copy-start(f32[4,512]{1,0:T(4,128)} %fields.1) | copy-start | bytes 24580
  0.0 1.7 %copy-start.3 = (f32[3,256]{1,0:T(4,128)S(1)}, f32[3,256]{1,0:T(4,128)}, u32[]{:S(2)}) copy-start(f32[3,256]{1,0:T(4,128)} %directions.1) | copy-start | bytes 9220
  1.7 0.7 %copy-start.4 = (f32[256]{0:T(256)S(1)}, f32[256]{0:T(256)}, u32[]{:S(2)}) copy-start(f32[256]{0:T(256)} %decay.1) | copy-start | bytes 3076

commit v3 on v2

--- a/solution.py
+++ b/solution.py
@@ -290,14 +290,19 @@
                 work.append(functools.partial(pair, 3, 0, 0, 1, 4, i))
                 work.append(functools.partial(pair, 4, 1, 0, 0, 4, i))
         for n, k in enumerate(order):
+            part_of = work[n * len(work) // count:(n + 1) * len(work) // count]
+            if s == STEPS - 1:
+                for task in part_of:
+                    task()
             if k == 0:
                 wait_y(s, 1)
                 wait_y(s, 2)
             x_copy(s, 0, k).wait()
             x_copy(s, 1, k).wait()
             boundary(s, k)
-            for task in work[n * len(work) // count:(n + 1) * len(work) // count]:
-                task()
+            if s + 1 < STEPS:
+                for task in part_of:
+                    task()
         if s + 1 < STEPS:
             send_y(s + 1, 1)
             send_y(s + 1, 2)

time: 38.3 us -> 38.3 us (level)
  no operation moved by 1% of the time
where the time goes in v3:
time: 38.3 us; the launch traced here: 38.1 us
  Pallas kernels  35.1 us (92%)
  local copies, waits for them, and re-layouts  2.92 us (8%)
    pallas_call x1, Pallas kernels, shards(): pl.pallas_call(functools.partial(kernel, devices, chunk), out_shape=jax.S...  35.1 us
    unnamed x12, local copies, waits for them, and re-layouts  2.92 us

profile of v3, /device:TPU:0, one launch (start us, length us, event | category | flops | bytes accessed | tf_op | source)
XLA Modules:
  0.0 38.1 jit_solution(17852886248760873479)
XLA Ops:
  0.0 0.0 copy-start.1
  0.0 0.0 copy-start
  0.0 0.0 copy-start.2
  0.0 0.0 copy-start.3
  0.0 1.7 %copy.7 = bf16[256,4,512]{0,2,1:T(8,128)(2,1)S(1)} copy(bf16[256,4,512]{2,1,0:T(4,128)(2,1)} %param.7) | data formatting | bytes 2097152 | tf_op args[1]
  1.7 0.0 copy-start.4
  1.7 0.0 copy-done.1
  1.7 0.0 copy-done
  1.7 0.0 copy-done.2
  1.7 0.0 copy-done.3
  1.7 0.6 %copy-done.4 = f32[256]{0:T(256)S(1)} copy-done((f32[256]{0:T(256)S(1)}, f32[256]{0:T(256)}, u32[]{:S(2)}) %copy-start.4) | copy-done | bytes 1048
  2.4 35.1 %propagate.1 = f32[4,512]{1,0:T(4,128)S(1)} custom-call(f32[4,512]{1,0:T(4,128)S(1)} %copy-done.2, bf16[4,512,256]{2,1,0:T(8,128)(2,1)S(1)} %bitcast.1, f32[3,256]{1,0:T(4,128)S(1)} %copy-done.3, bf16[256,256]{1,0:T(8,128)(2,1)S(1)} %copy-done, bf16[256,256]{1,0:T(8,128)(2,1)S(1)} %copy-done.1, f32[256]{0:T(256)S(1)} %copy-done.4), custom_call_target="tpu_custom_call" | custom-call | tf_op jit(solution)/shard_map/propagate/pallas_call | solution.py:343
  37.5 0.6 %copy.9 = f32[4,512]{1,0:T(4,128)} copy(f32[4,512]{1,0:T(4,128)S(1)} %propagate.1) | data formatting | bytes 16384
Async XLA Ops:
  0.0 1.7 %copy-start.1 = (bf16[256,256]{1,0:T(8,128)(2,1)S(1)}, bf16[256,256]{1,0:T(8,128)(2,1)}, u32[]{:S(2)}) copy-start(bf16[256,256]{1,0:T(8,128)(2,1)} %synthesis.1) | copy-start | bytes 393220
  0.0 1.7 %copy-start = (bf16[256,256]{1,0:T(8,128)(2,1)S(1)}, bf16[256,256]{1,0:T(8,128)(2,1)}, u32[]{:S(2)}) copy-start(bf16[256,256]{1,0:T(8,128)(2,1)} %analysis.1) | copy-start | bytes 393220
  0.0 1.7 %copy-start.2 = (f32[4,512]{1,0:T(4,128)S(1)}, f32[4,512]{1,0:T(4,128)}, u32[]{:S(2)}) copy-start(f32[4,512]{1,0:T(4,128)} %fields.1) | copy-start | bytes 24580
  0.0 1.7 %copy-start.3 = (f32[3,256]{1,0:T(4,128)S(1)}, f32[3,256]{1,0:T(4,128)}, u32[]{:S(2)}) copy-start(f32[3,256]{1,0:T(4,128)} %directions.1) | copy-start | bytes 9220
  1.7 0.7 %copy-start.4 = (f32[256]{0:T(256)S(1)}, f32[256]{0:T(256)}, u32[]{:S(2)}) copy-start(f32[256]{0:T(256)} %decay.1) | copy-start | bytes 3076
